TPU v7x, 32 devices: a whole 2x2x4 slice. The times are simulated.
32 devices in a mesh: req: 4 (over z), row: 4 (over y, core), col: 2 (over x).
Axes of the slice: x: 2, y: 2, z: 4, core: 2. Of those that a mesh axis runs over, the one named last changes fastest.
Arguments:
- hidden: bfloat16 [1024, 2048], P(('req', 'row')), may hold values from -6 to 6
- latent_cache: bfloat16 [16, 384, 576], P('req'), may hold values from -144 to 144
- lengths: int32 [16], P('req'), may hold values from 96 to 384
- parents: int32 [16, 64], P('req'), may hold values from -1 to 62, as said below
- routes: int32 [1024, 6], P(('req', 'row')), may hold values from 0 to 15, all different within a row; in each aligned block of 64 rows (0 to 63, 64 to 127, ...) at most 48 rows name the same one
- accepted: int32 [16], P(('req', 'row')), may hold values from 0 to 63
- input_gain: float32 [2048], replicated, may hold values from 0.25 to 1.75
- query_weight: bfloat16 [2048, 3072], P(None, ('row', 'col')), may hold values from -0.125 to 0.125
- latent_weight: bfloat16 [2048, 576], replicated, may hold values from -0.125 to 0.125
- latent_gain: float32 [512], replicated, may hold values from 0.25 to 1.75
- key_absorb: bfloat16 [16, 128, 512], P(('row', 'col')), may hold values from -0.5 to 0.5
- value_absorb: bfloat16 [16, 512, 128], P(('row', 'col')), may hold values from -0.25 to 0.25
- output_weight: bfloat16 [2048, 2048], P(('row', 'col')), may hold values from -0.125 to 0.125
- post_gain: float32 [2048], replicated, may hold values from 0.25 to 1.75
- router_weight: bfloat16 [2048, 16], replicated, may hold values from -0.046875 to 0.046875
- shared_gate_up: bfloat16 [2, 2048, 2816], P(None, None, ('row', 'col')), may hold values from -0.125 to 0.125
- shared_down: bfloat16 [2816, 2048], P(('row', 'col')), may hold values from -0.109375 to 0.109375
- expert_gate_up: bfloat16 [16, 2, 2048, 1408], P(('req', 'row'), None, None, 'col'), may hold values from -0.125 to 0.125
- expert_down: bfloat16 [16, 1408, 2048], P(('req', 'row'), 'col'), may hold values from -1.5 to 1.5
Outputs:
- layer_output: bfloat16 [1024, 2048], P(('req', 'row'))
- accepted_latents: bfloat16 [16, 64, 576], P(('req', 'row'))
Inputs may be any that keep to these rules, and one draw needn't show every extreme that they name: parents[r, 0] is -1 and parents[r, i] lies in 0 to i - 1 for i >= 1. `routes`: the 6 experts of a token differ; within the 64 rows of one index of req and row no expert is named by more than 48 rows.
All inputs are finite; a program needn't handle non-finite values.
Results may differ from a plain program's by a relative error of at most 0.009.
The roundings to bfloat16 on the way count: a program that leaves them out, or rounds other values in their place, can miss the bound.
Values may be sent and summed in bfloat16 or wider, within the bound.
No kernel may reach another device: no remote copies, remote signals or barrier semaphores. Data moves between devices by JAX's collectives and lax.ppermute only.
A program may use at most 128 MiB of HBM per device.

v0:
```python
import math
import jax
import jax.numpy as jnp
from jax import lax
from jax.sharding import PartitionSpec as P

NOPE = 128
ROPE = 64
LAT = 512
VDIM = 128
CACHE = 384
WINDOW = 160
SINK = 4
EPSILON = 1e-06


def rms_scale(values, gain_row):
    mean_square = jnp.mean(values * values, axis=-1, keepdims=True)
    return values * lax.rsqrt(mean_square + EPSILON) * gain_row


def rope_tables(positions, rope_width):
    half_width = rope_width // 2
    frequency = jnp.exp(
        jnp.arange(half_width, dtype=jnp.float32) * (-2.0 * math.log(10000.0) / rope_width)
    )
    angles = positions[..., None] * frequency
    return (jnp.cos(angles), jnp.sin(angles))


def rotate(values, cosine, sine_part):
    half_width = values.shape[-1] // 2
    first_half = values[..., :half_width]
    second_half = values[..., half_width:]
    return jnp.concatenate(
        [
            first_half * cosine - second_half * sine_part,
            second_half * cosine + first_half * sine_part,
        ],
        axis=-1,
    )


def ancestry(parents):
    tree_size = parents.shape[-1]
    node_ids = jnp.arange(tree_size, dtype=jnp.int32)
    links = (parents[..., :, None] == node_ids[None, :]).astype(jnp.float32)
    closure = links + jnp.eye(tree_size, dtype=jnp.float32)
    for repeat in range(max(1, (tree_size - 1).bit_length())):
        closure = jnp.minimum(
            jnp.einsum("...ij,...jk->...ik", closure, closure, precision=lax.Precision.HIGHEST), 1.0
        )
    depths = jnp.sum(closure, axis=-1) - 1.0
    return (closure, depths)


def gather_rows(values):
    return lax.all_gather(values, "row", axis=0, tiled=True)


def project_down(values, weight):
    return lax.psum_scatter(
        jnp.dot(values, weight, preferred_element_type=jnp.float32),
        "row",
        scatter_dimension=0,
        tiled=True,
    )


def col_total(values):
    return lax.psum(values, "col")


def body(
    hidden,
    latent_cache,
    lengths,
    parents,
    routes,
    accepted,
    input_gain,
    query_weight,
    latent_weight,
    latent_gain,
    key_absorb,
    value_absorb,
    output_weight,
    post_gain,
    router_weight,
    shared_gate_up,
    shared_down,
    expert_gate_up,
    expert_down,
):
    tok_rows = hidden.shape[0]
    model_width = hidden.shape[1]
    group_reqs, tree_size = parents.shape
    head_count = key_absorb.shape[0]
    scale_factor = 1.0 / math.sqrt(NOPE + ROPE)
    normed = rms_scale(hidden.astype(jnp.float32), input_gain).astype(jnp.bfloat16)
    group_rows = gather_rows(normed)
    closure, depths = ancestry(parents)
    queries = jnp.dot(group_rows, query_weight, preferred_element_type=jnp.float32).astype(
        jnp.bfloat16
    )
    queries = queries.reshape(group_reqs, tree_size, head_count, NOPE + ROPE)
    projected = jnp.dot(group_rows, latent_weight, preferred_element_type=jnp.float32).reshape(
        group_reqs, tree_size, LAT + ROPE
    )
    positions = lengths.astype(jnp.float32)[:, None] + depths
    cosine, sine_part = rope_tables(positions, ROPE)
    content = rms_scale(projected[..., :LAT], latent_gain)
    key_rope = rotate(projected[..., LAT:], cosine, sine_part)
    fresh_latents = jnp.concatenate([content, key_rope], axis=-1).astype(jnp.bfloat16)
    query_latent = jnp.einsum(
        "rthn,hnl->rthl", queries[..., :NOPE], key_absorb, preferred_element_type=jnp.float32
    ).astype(jnp.bfloat16)
    query_rope = rotate(
        queries[..., NOPE:].astype(jnp.float32), cosine[:, :, None, :], sine_part[:, :, None, :]
    ).astype(jnp.bfloat16)
    query_full = jnp.concatenate([query_latent, query_rope], axis=-1)
    key_rows = jnp.concatenate([latent_cache, fresh_latents], axis=1)
    scores = (
        jnp.einsum("rthc,rkc->rhtk", query_full, key_rows, preferred_element_type=jnp.float32)
        * scale_factor
    )
    cache_spots = jnp.arange(CACHE, dtype=jnp.int32)[None, :]
    length_col = lengths[:, None]
    cache_allowed = (cache_spots < length_col) & (
        (cache_spots < SINK) | (cache_spots >= length_col - WINDOW)
    )
    allowed = jnp.concatenate(
        [
            jnp.broadcast_to(cache_allowed[:, None, :], (group_reqs, tree_size, CACHE)),
            closure > 0.5,
        ],
        axis=-1,
    )
    scores = jnp.where(allowed[:, None], scores, -1e30)
    row_peak = jnp.max(scores, axis=-1, keepdims=True)
    weights = jnp.exp(scores - row_peak)
    attention_weights = (weights / jnp.sum(weights, axis=-1, keepdims=True)).astype(jnp.bfloat16)
    out_latent = jnp.einsum(
        "rhtk,rkl->rthl", attention_weights, key_rows[..., :LAT], preferred_element_type=jnp.float32
    ).astype(jnp.bfloat16)
    head_output = jnp.einsum(
        "rthl,hlv->rthv", out_latent, value_absorb, preferred_element_type=jnp.float32
    ).astype(jnp.bfloat16)
    head_rows = head_output.reshape(group_reqs * tree_size, head_count * VDIM)
    attention_part = project_down(head_rows, output_weight)
    residual = hidden.astype(jnp.float32) + col_total(attention_part)
    post_normed = rms_scale(residual, post_gain).astype(jnp.bfloat16)
    router = jax.nn.softmax(
        jnp.dot(post_normed, router_weight, preferred_element_type=jnp.float32), axis=-1
    )
    experts = router_weight.shape[1]
    top_count = routes.shape[1]
    capacity = min(tok_rows, max(2, 2 * tok_rows * top_count // experts))
    labels = jnp.arange(experts, dtype=jnp.int32)
    chosen = jnp.sum((routes[:, :, None] == labels[None, None, :]).astype(jnp.float32), axis=1)
    row_order = jnp.arange(tok_rows, dtype=jnp.int32)
    earlier = (row_order[None, :] < row_order[:, None]).astype(jnp.float32)
    slot_rank = jnp.dot(earlier, chosen, precision=lax.Precision.HIGHEST)
    slot_ids = jnp.arange(capacity, dtype=jnp.float32)
    placing = (chosen.T[:, None, :] > 0.5) & (slot_rank.T[:, None, :] == slot_ids[None, :, None])
    outbound = jnp.einsum(
        "est,td->esd", placing.astype(jnp.bfloat16), post_normed, preferred_element_type=jnp.float32
    ).astype(jnp.bfloat16)
    inbound = lax.all_to_all(outbound, ("req", "row"), split_axis=0, concat_axis=0, tiled=True)
    group_post = gather_rows(post_normed)
    shared_gate = jnp.dot(group_post, shared_gate_up[0], preferred_element_type=jnp.float32)
    shared_upper = jnp.dot(group_post, shared_gate_up[1], preferred_element_type=jnp.float32)
    shared_hidden = (jax.nn.silu(shared_gate) * shared_upper).astype(jnp.bfloat16)
    shared_part = project_down(shared_hidden, shared_down)
    sources = inbound.shape[0]
    slot_rows = inbound.reshape(sources * capacity, model_width)
    expert_gate = jnp.dot(slot_rows, expert_gate_up[0, 0], preferred_element_type=jnp.float32)
    expert_upper = jnp.dot(slot_rows, expert_gate_up[0, 1], preferred_element_type=jnp.float32)
    expert_hidden = (jax.nn.silu(expert_gate) * expert_upper).astype(jnp.bfloat16)
    expert_result = jnp.dot(
        expert_hidden, expert_down[0], preferred_element_type=jnp.float32
    ).reshape(sources, capacity, model_width)
    returned = lax.all_to_all(
        expert_result.astype(jnp.bfloat16), ("req", "row"), split_axis=0, concat_axis=0, tiled=True
    ).astype(expert_result.dtype)
    weighting = placing.astype(jnp.float32) * router.T[:, None, :]
    routed = jnp.einsum("est,esd->td", weighting, returned, precision=lax.Precision.HIGHEST)
    summed_parts = col_total(shared_part + routed)
    layer_output = (residual + summed_parts).astype(jnp.bfloat16)
    own_count = accepted.shape[0]
    own_start = lax.axis_index("row") * own_count
    own_closure = lax.dynamic_slice_in_dim(closure, own_start, own_count, 0)
    own_depths = lax.dynamic_slice_in_dim(depths, own_start, own_count, 0)
    own_fresh = lax.dynamic_slice_in_dim(fresh_latents, own_start, own_count, 0)
    chooser = (jnp.arange(tree_size, dtype=jnp.int32)[None, :] == accepted[:, None]).astype(
        jnp.float32
    )
    path_mask = jnp.einsum("qi,qij->qj", chooser, own_closure, precision=lax.Precision.HIGHEST)
    levels = jnp.arange(tree_size, dtype=jnp.float32)
    path_places = path_mask[:, None, :] * (own_depths[:, None, :] == levels[None, :, None]).astype(
        jnp.float32
    )
    accepted_latents = jnp.einsum(
        "qkj,qjc->qkc",
        path_places.astype(jnp.bfloat16),
        own_fresh,
        preferred_element_type=jnp.float32,
    ).astype(jnp.bfloat16)
    return (layer_output, accepted_latents)


def solution(mesh):
    placed = (
        P(("req", "row"), None),
        P("req", None, None),
        P("req"),
        P("req", None),
        P(("req", "row"), None),
        P(("req", "row")),
        P(),
        P(None, ("row", "col")),
        P(),
        P(),
        P(("row", "col"), None, None),
        P(("row", "col"), None, None),
        P(("row", "col"), None),
        P(),
        P(),
        P(None, None, ("row", "col")),
        P(("row", "col"), None),
        P(("req", "row"), None, None, "col"),
        P(("req", "row"), "col", None),
    )
    return jax.shard_map(
        body,
        mesh=mesh,
        in_specs=placed,
        out_specs=(P(("req", "row"), None), P(("req", "row"), None, None)),
        check_vma=False,
    )
```

profile of v0, /device:TPU:0, one launch (start us, length us, event | category | flops | bytes accessed | tf_op | source)
XLA Modules:
  0.0 329.5 jit_solution(12373238078999165010)
XLA Ops:
  7.2 1.3 fusion.52
  8.5 1.8 fusion.54
  10.4 0.7 broadcast_add_fusion.2
  11.1 1.1 convolution_minimum_fusion.5
  12.2 0.3 convolution_minimum_fusion.4
  12.5 3.9 %copy.34 = bf16[4,384,576]{2,1,0:T(8,128)(2,1)} copy(bf16[4,384,576]{1,2,0:T(8,128)(2,1)} %param.20) | data formatting | bytes 3538944 | tf_op args[1]
  16.5 0.3 convolution_minimum_fusion.3
  16.8 0.3 convolution_minimum_fusion.2
  17.0 0.3 convolution_minimum_fusion.1
  17.3 0.4 fusion.110
  17.7 0.7 pad_add_fusion
  18.4 0.6 broadcast_add_fusion
  19.0 11.0 %all-gather.3.cloned.1.call-done = bf16[256,2048]{1,0:T(8,128)(2,1)} async-done(((bf16[64,2048]{1,0:T(8,128)(2,1)}), bf16[256,2048]{1,0:T(8,128)(2,1)}) %all-gather.3.cloned.1.call-update) | async-done | bytes 1048592 | tf_op jit(solution)/shard_map/all_gather | solution.py:58
  30.0 2.4 convolution_convert_fusion.3
  32.4 0.2 reshape.209
  32.7 3.0 fusion.117
  36.1 0.6 multiply_cosine_fusion
  36.7 0.8 slice-done
  37.5 1.1 fusion.32
  38.5 0.8 subtract_convert_fusion
  39.3 1.7 maximum_maximum_fusion
  41.0 3.8 %fusion.111 = (f32[4,2,64]{2,1,0:T(2,128)S(1)}, f32[4,2,64,448]{3,2,1,0:T(8,128)}) fusion(bf16[4,448,576]{2,1,0:T(8,128)(2,1)} %maximum_maximum_fusion, bf16[4,64,2,32]{3,1,2,0:T(8,128)(2,1)} %get-tuple-element.5, bf16[4,64,2,32]{3,1,2,0:T(8,128)(2,1)S(1)} %get-tuple-element.4, bf16[4,64,2,512]{3,1,2,0:T(8,128)(2,1)} %fusion.32, ...), kind=kOutput, calls=%fused_computation.152 | convolution fusion | flops 266928576 | bytes 3688448 | tf_op jit(solution)/shard_map/sub | solution.py:141
  44.8 2.5 fusion.45
  47.5 3.1 fusion.76
  50.6 31.5 %reduce-scatter.3.cloned.1.call-done = f32[64,2048]{1,0:T(8,128)} async-done(((f32[256,2048]{1,0:T(8,128)}), f32[64,2048]{1,0:T(8,128)}) %reduce-scatter.3.cloned.1.call-update) | async-done | bytes 524304 | tf_op jit(solution)/shard_map/reduce_scatter | solution.py:62
  82.3 30.8 %all-reduce.3.cloned.1.call-done = f32[64,2048]{1,0:T(8,128)} async-done(((f32[64,2048]{1,0:T(8,128)}), f32[64,2048]{1,0:T(8,128)}) %all-reduce.3.cloned.1.call-update) | async-done | bytes 524304 | tf_op jit(solution)/shard_map/psum | solution.py:71
  113.1 1.2 multiply_reduce_fusion
  114.3 1.2 multiply_convert_fusion.1
  115.5 2.7 convolution_convert_fusion.1
  118.2 5.7 %all-to-all-start = ((bf16[16,48,2048]{2,1,0:T(8,128)(2,1)}), bf16[16,48,2048]{2,1,0:T(8,128)(2,1)}, u32[]{:S(2)}, u32[]{:S(2)}) async-start(bf16[16,48,2048]{2,1,0:T(8,128)(2,1)} %convolution_convert_fusion.1), calls=%async_computation.2 | async-start | bytes 6291456 | tf_op jit(solution)/shard_map/all_to_all | solution.py:169
  123.9 0.2 all-gather.5.cloned.1.call-start
  124.1 0.3 all-gather.5.cloned.1.call-update
  124.5 58.9 %all-to-all-done = bf16[16,48,2048]{2,1,0:T(8,128)(2,1)} async-done(((bf16[16,48,2048]{2,1,0:T(8,128)(2,1)}), bf16[16,48,2048]{2,1,0:T(8,128)(2,1)}, u32[]{:S(2)}, u32[]{:S(2)}) %all-to-all-start) | async-done | bytes 3145760 | tf_op jit(solution)/shard_map/all_to_all | solution.py:169
  183.3 5.2 %fusion.4 = f32[768,704]{0,1:T(8,128)S(1)} fusion(bf16[768,2048]{1,0:T(8,128)(2,1)} %bitcast.16, bf16[1,2,2048,704]{2,3,1,0:T(8,128)(2,1)} %param.36), kind=kOutput, calls=%fused_computation.6 | convolution fusion | flops 2214592512 | bytes 8192000 | tf_op jit(solution)/shard_map/dot_general | solution.py:177
  188.6 6.3 %multiply_convert_fusion = bf16[768,704]{0,1:T(8,128)(2,1)} fusion(f32[768,704]{0,1:T(8,128)S(1)} %fusion.4, bf16[768,2048]{1,0:T(8,128)(2,1)} %bitcast.16, bf16[1,2,2048,704]{2,3,1,0:T(8,128)(2,1)} %param.36), kind=kOutput, calls=%fused_computation.15 | convolution fusion | flops 2217836544 | bytes 9273344 | tf_op jit(solution)/shard_map/dot_general | solution.py:178
  194.9 2.4 copy.39
  197.3 5.3 %convolution_convert_fusion = bf16[16,48,2048]{2,1,0:T(8,128)(2,1)} fusion(bf16[16,48,704]{2,1,0:T(8,128)(2,1)} %bitcast.141, bf16[1,704,2048]{2,1,0:T(8,128)(2,1)S(1)} %copy-done), kind=kOutput, calls=%fused_computation.1 | convolution fusion | flops 2216165376 | bytes 7110656 | tf_op jit(solution)/shard_map/dot_general | solution.py:180
  202.6 15.5 %all-to-all-start.1 = ((bf16[16,48,2048]{2,1,0:T(8,128)(2,1)}), bf16[16,48,2048]{2,1,0:T(8,128)(2,1)}, u32[]{:S(2)}, u32[]{:S(2)}) async-start(bf16[16,48,2048]{2,1,0:T(8,128)(2,1)} %convolution_convert_fusion), calls=%async_computation.3 | async-start | bytes 6291456 | tf_op jit(solution)/shard_map/all_to_all | solution.py:183
  218.2 3.0 fusion.17
  221.2 5.7 %fusion.43 = f32[256,2048]{1,0:T(8,128)} fusion(bf16[352,2048]{1,0:T(8,128)(2,1)} %param.35, bf16[256,2048]{1,0:T(8,128)(2,1)} %all-gather.5.cloned.1.call-done, bf16[2,2048,352]{1,2,0:T(8,128)(2,1)} %param.34, f32[256,352]{0,1:T(8,128)} %fusion.17), kind=kOutput, calls=%fused_computation.38 | convolution fusion | flops 738738176 | bytes 6389760 | tf_op jit(solution)/shard_map/dot_general | solution.py:63
  226.9 1.0 fusion.112
  228.0 38.3 %reduce-scatter.5.cloned.1.call-done = f32[64,2048]{1,0:T(8,128)} async-done(((f32[256,2048]{1,0:T(8,128)}), f32[64,2048]{1,0:T(8,128)}) %reduce-scatter.5.cloned.1.call-update) | async-done | bytes 524304 | tf_op jit(solution)/shard_map/reduce_scatter | solution.py:62
  266.3 11.3 %all-to-all-done.1 = bf16[16,48,2048]{2,1,0:T(8,128)(2,1)} async-done(((bf16[16,48,2048]{2,1,0:T(8,128)(2,1)}), bf16[16,48,2048]{2,1,0:T(8,128)(2,1)}, u32[]{:S(2)}, u32[]{:S(2)}) %all-to-all-start.1) | async-done | bytes 3145760 | tf_op jit(solution)/shard_map/all_to_all | solution.py:183
  277.6 4.6 %fusion.8 = f32[64,2048]{1,0:T(8,128)} fusion(f32[64,2048]{1,0:T(8,128)} %reduce-scatter.5.cloned.1.call-done, bf16[16,48,2048]{2,1,0:T(8,128)(2,1)} %all-to-all-done.1, f32[16,64]{1,0:T(8,128)S(1)} %divide_bitcast_fusion, f32[16,64]{1,0:T(8,128)S(1)} %fusion.91, pred[16,64]{1,0:T(8,128)(4,1)} %copy-done.12), kind=kOutput, calls=%fused_computation.11 | convolution fusion | flops 1208238080 | bytes 4203520 | tf_op jit(solution)/shard_map/est,esd->td/dot_general | solution.py:187
  283.0 0.7 fusion.102
  283.7 1.6 fusion.46
  285.3 35.4 %all-reduce.5.cloned.1.call-done = f32[64,2048]{1,0:T(8,128)} async-done(((f32[64,2048]{1,0:T(8,128)}), f32[64,2048]{1,0:T(8,128)}) %all-reduce.5.cloned.1.call-update) | async-done | bytes 524304 | tf_op jit(solution)/shard_map/psum | solution.py:71
  320.7 2.0 add_convert_fusion
  (64 shorter events, 1.4 us)
Async XLA Ops:
  7.2 190.1 %copy-start = (bf16[1,704,2048]{2,1,0:T(8,128)(2,1)S(1)}, bf16[1,704,2048]{2,1,0:T(8,128)(2,1)}, u32[]{:S(2)}) copy-start(bf16[1,704,2048]{2,1,0:T(8,128)(2,1)} %param.37) | copy-start | bytes 8650756
  7.2 22.8 %all-gather.3.cloned.1.call-start = ((), (), s32[]{:S(2)}) async-start(), calls=%async_computation.4 | async-start | bytes 1310720 | tf_op jit(solution)/shard_map/all_gather | solution.py:58
  10.3 6.1 %copy-start.15 = (s32[4]{0:T(128)S(1)}, s32[4]{0:T(128)}, u32[]{:S(2)}) copy-start(s32[4]{0:T(128)} %param.21) | copy-start | bytes 52
  10.3 71.8 %reduce-scatter.3.cloned.1.call-start = ((), (), s32[]{:S(2)}) async-start(), calls=%async_computation.5 | async-start | bytes 2621440 | tf_op jit(solution)/shard_map/reduce_scatter | solution.py:62
  32.6 3.1 copy-start.7
  32.7 3.2 copy-start.14
  35.7 1.0 copy-start.10
  35.8 3.6 %copy-start.1 = (bf16[4,384,576]{2,1,0:T(8,128)(2,1)S(1)}, bf16[4,384,576]{2,1,0:T(8,128)(2,1)}, u32[]{:S(2)}) copy-start(bf16[4,384,576]{2,1,0:T(8,128)(2,1)} %copy.34) | copy-start | bytes 5308420
  35.8 1.7 slice-start
  36.1 4.9 %copy-start.5 = (bf16[4,64,512]{2,1,0:T(8,128)(2,1)}, bf16[4,64,512]{2,1,0:T(8,128)(2,1)S(1)}, u32[]{:S(2)}) copy-start(bf16[4,64,512]{2,1,0:T(8,128)(2,1)S(1)} %multiply_convert_fusion.2) | copy-start | bytes 786436
  37.5 3.5 %copy-start.8 = (bf16[4,64,32]{2,1,0:T(8,128)(2,1)}, bf16[4,64,32]{2,1,0:T(8,128)(2,1)S(1)}, u32[]{:S(2)}) copy-start(bf16[4,64,32]{2,1,0:T(8,128)(2,1)S(1)} %get-tuple-element.8) | copy-start | bytes 49156
  37.5 3.5 %copy-start.9 = (bf16[4,64,32]{2,1,0:T(8,128)(2,1)}, bf16[4,64,32]{2,1,0:T(8,128)(2,1)S(1)}, u32[]{:S(2)}) copy-start(bf16[4,64,32]{2,1,0:T(8,128)(2,1)S(1)} %get-tuple-element.9) | copy-start | bytes 49156
  39.3 1.7 copy-start.11
  47.4 34.7 %copy-start.13 = (s32[64,6]{0,1:T(8,128)S(1)}, s32[64,6]{0,1:T(8,128)}, u32[]{:S(2)}) copy-start(s32[64,6]{0,1:T(8,128)} %param.23) | copy-start | bytes 4612
  47.4 65.7 %copy-start.2 = (bf16[64,2048]{1,0:T(8,128)(2,1)S(1)}, bf16[64,2048]{1,0:T(8,128)(2,1)}, u32[]{:S(2)}) copy-start(bf16[64,2048]{1,0:T(8,128)(2,1)} %param.19) | copy-start | bytes 786436
  50.5 62.6 %all-reduce.3.cloned.1.call-start = ((), (), s32[]{:S(2)}) async-start(), calls=%async_computation.6 | async-start | bytes 1048576 | tf_op jit(solution)/shard_map/psum | solution.py:71
  82.1 36.1 %copy-start.12 = (pred[16,64]{1,0:T(8,128)(4,1)}, pred[16,64]{1,0:T(8,128)(4,1)S(1)}, u32[]{:S(2)}) copy-start(pred[16,64]{1,0:T(8,128)(4,1)S(1)} %compare_bitcast_fusion) | copy-start | bytes 3076
  115.5 2.7 copy-start.3
  118.2 65.1 %all-to-all-start = ((bf16[16,48,2048]{2,1,0:T(8,128)(2,1)}), bf16[16,48,2048]{2,1,0:T(8,128)(2,1)}, u32[]{:S(2)}, u32[]{:S(2)}) async-start(bf16[16,48,2048]{2,1,0:T(8,128)(2,1)} %convolution_convert_fusion.1), calls=%async_computation.2 | async-start | bytes 6291456 | tf_op jit(solution)/shard_map/all_to_all | solution.py:169
  123.9 94.3 %all-gather.5.cloned.1.call-start = ((), (), s32[]{:S(2)}) async-start(), calls=%async_computation.7 | async-start | bytes 1310720 | tf_op jit(solution)/shard_map/all_gather | solution.py:58
  202.6 75.0 %all-to-all-start.1 = ((bf16[16,48,2048]{2,1,0:T(8,128)(2,1)}), bf16[16,48,2048]{2,1,0:T(8,128)(2,1)}, u32[]{:S(2)}, u32[]{:S(2)}) async-start(bf16[16,48,2048]{2,1,0:T(8,128)(2,1)} %convolution_convert_fusion), calls=%async_computation.3 | async-start | bytes 6291456 | tf_op jit(solution)/shard_map/all_to_all | solution.py:183
  218.1 48.3 %reduce-scatter.5.cloned.1.call-start = ((), (), s32[]{:S(2)}) async-start(), calls=%async_computation.8 | async-start | bytes 2621440 | tf_op jit(solution)/shard_map/reduce_scatter | solution.py:62
  221.2 5.7 %copy-start.4 = (bf16[64,2048]{1,0:T(8,128)(2,1)S(1)}, bf16[64,2048]{1,0:T(8,128)(2,1)}, u32[]{:S(2)}) copy-start(bf16[64,2048]{1,0:T(8,128)(2,1)} %copy-done.3) | copy-start | bytes 786436
  226.9 93.9 %all-reduce.5.cloned.1.call-start = ((), (), s32[]{:S(2)}) async-start(), calls=%async_computation.9 | async-start | bytes 1048576 | tf_op jit(solution)/shard_map/psum | solution.py:71
  228.0 55.7 %copy-start.6 = (bf16[4,64,512]{2,1,0:T(8,128)(2,1)S(1)}, bf16[4,64,512]{2,1,0:T(8,128)(2,1)}, u32[]{:S(2)}) copy-start(bf16[4,64,512]{2,1,0:T(8,128)(2,1)} %copy-done.5) | copy-start | bytes 786436
Sparse Core Ops, SparseCore 0:
  10.4 19.5 all-gather.2
  50.7 31.3 reduce-scatter.2
  84.5 28.5 all-reduce.2
  126.5 30.3 all-gather.4
  227.0 39.3 reduce-scatter.4
  282.4 38.2 all-reduce.4
where the time goes:
time: 330 us
  waiting for transfers between devices  218 us (66%)
  matrix products  54 us (16%)
  starting transfers between devices  21.6 us (7%)
  between operations  15.1 us (5%)
  other arithmetic  12.9 us (4%)
  local copies, waits for them, and re-layouts  8.26 us (3%)
    reduce_scatter x2, waiting for transfers between devices, project_down(): lax.psum_scatter(jnp.dot(values, weight, preferred_element_type=jnp.float...  69.8 us
    psum x2, waiting for transfers between devices, col_total(): return lax.psum(values, 'col')  66.2 us
    all_to_all x1, waiting for transfers between devices, body(): lax.all_to_all(outbound, ('req', 'row'), split_axis=0, concat_axis=0, til...  58.9 us
    all_to_all x1, starting transfers between devices, body(): lax.all_to_all(expert_result.astype(jnp.bfloat16), ('req', 'row'), split_...  15.5 us
    all_to_all x1, waiting for transfers between devices, body(): lax.all_to_all(expert_result.astype(jnp.bfloat16), ('req', 'row'), split_...  11.3 us
    all_gather x2, waiting for transfers between devices, gather_rows(): return lax.all_gather(values, 'row', axis=0, tiled=True)  11 us
    dot_general x2, matrix products, project_down(): jnp.dot(values, weight, preferred_element_type=jnp.float32)  8.71 us
  transfers between devices with their start and end apart: 8, of which 7 were waited for; matrix products, arithmetic and copies ran while one was open for 12% of the time, Pallas kernels for 0%

commit v1 on v0

--- a/solution.py
+++ b/solution.py
@@ -68,7 +68,7 @@
 
 
 def col_total(values):
-    return lax.psum(values, "col")
+    return jnp.sum(lax.all_gather(values, "col"), axis=0)
 
 
 def body(

time: 330 us -> 319 us (0.967)
  waiting for transfers between devices: 218 us -> 202 us
  other arithmetic: 12.9 us -> 16.9 us
    psum x2 -> x0, waiting for transfers between devices: 66.2 us -> none  [col_total(): return lax.psum(values, 'col')]
    all_gather x0 -> x2, waiting for transfers between devices: none -> 50.8 us  [col_total(): return jnp.sum(lax.all_gather(values, 'col'), axis=0)]
    reduce_sum x0 -> x2, other arithmetic: none -> 3.49 us  [col_total(): return jnp.sum(lax.all_gather(values, 'col'), axis=0)]
  transfers between devices with their start and end apart: 8 -> 8, of which waited for: 7 -> 7; matrix products, arithmetic and copies ran while one was open for 12% -> 13% of each run, Pallas kernels for 0% -> 0%
where the time goes in v1:
time: 319 us; the launch traced here: 318 us
  waiting for transfers between devices  202 us (63%)
  matrix products  54.1 us (17%)
  starting transfers between devices  21.6 us (7%)
  other arithmetic  16.9 us (5%)
  between operations  15.1 us (5%)
  local copies, waits for them, and re-layouts  8.24 us (3%)
    reduce_scatter x2, waiting for transfers between devices, project_down(): lax.psum_scatter(jnp.dot(values, weight, preferred_element_type=jnp.float...  69.8 us
    all_to_all x1, waiting for transfers between devices, body(): lax.all_to_all(outbound, ('req', 'row'), split_axis=0, concat_axis=0, til...  58.9 us
    all_gather x2, waiting for transfers between devices, col_total(): return jnp.sum(lax.all_gather(values, 'col'), axis=0)  50.8 us
    all_to_all x1, starting transfers between devices, body(): lax.all_to_all(expert_result.astype(jnp.bfloat16), ('req', 'row'), split_...  15.5 us
    all_to_all x1, waiting for transfers between devices, body(): lax.all_to_all(expert_result.astype(jnp.bfloat16), ('req', 'row'), split_...  11.3 us
    all_gather x2, waiting for transfers between devices, gather_rows(): return lax.all_gather(values, 'row', axis=0, tiled=True)  11 us
    dot_general x2, matrix products, project_down(): jnp.dot(values, weight, preferred_element_type=jnp.float32)  8.6 us
  transfers between devices with their start and end apart: 8, of which 7 were waited for; matrix products, arithmetic and copies ran while one was open for 13% of the time, Pallas kernels for 0%

profile of v1, /device:TPU:0, one launch (start us, length us, event | category | flops | bytes accessed | tf_op | source)
XLA Modules:
  0.0 318.1 jit_solution(13013918573702020785)
XLA Ops:
  7.2 1.3 fusion.52
  8.5 1.8 fusion.54
  10.4 0.7 broadcast_add_fusion.2
  11.1 1.1 convolution_minimum_fusion.5
  12.3 0.3 convolution_minimum_fusion.4
  12.5 3.9 %copy.34 = bf16[4,384,576]{2,1,0:T(8,128)(2,1)} copy(bf16[4,384,576]{1,2,0:T(8,128)(2,1)} %param.20) | data formatting | bytes 3538944 | tf_op args[1]
  16.5 0.3 convolution_minimum_fusion.3
  16.8 0.3 convolution_minimum_fusion.2
  17.0 0.3 convolution_minimum_fusion.1
  17.3 0.4 fusion.110
  17.7 0.7 pad_add_fusion
  18.4 0.6 broadcast_add_fusion
  19.0 11.0 %all-gather.7.cloned.1.call-done = bf16[256,2048]{1,0:T(8,128)(2,1)} async-done(((bf16[64,2048]{1,0:T(8,128)(2,1)}), bf16[256,2048]{1,0:T(8,128)(2,1)}) %all-gather.7.cloned.1.call-update) | async-done | bytes 1048592 | tf_op jit(solution)/shard_map/all_gather | solution.py:58
  30.0 2.4 convolution_convert_fusion.3
  32.7 3.0 fusion.117
  36.1 0.6 multiply_cosine_fusion
  36.7 0.8 slice-done
  37.5 0.3 fusion.32
  37.8 0.8 subtract_convert_fusion
  38.6 1.7 maximum_maximum_fusion
  40.3 3.7 %fusion.111 = (f32[4,2,64]{2,1,0:T(2,128)S(1)}, f32[4,2,64,448]{3,2,1,0:T(8,128)}) fusion(bf16[4,448,576]{2,1,0:T(8,128)(2,1)} %maximum_maximum_fusion, bf16[4,64,2,32]{3,1,2,0:T(8,128)(2,1)} %get-tuple-element.5, bf16[4,64,2,32]{3,1,2,0:T(8,128)(2,1)} %get-tuple-element.4, bf16[4,64,2,512]{3,1,2,0:T(8,128)(2,1)S(1)} %fusion.32, ...), kind=kOutput, calls=%fused_computation.152 | convolution fusion | flops 266928576 | bytes 3688448 | tf_op jit(solution)/shard_map/sub | solution.py:141
  43.9 2.5 fusion.45
  46.6 3.0 fusion.76
  49.7 31.5 %reduce-scatter.3.cloned.1.call-done = f32[64,2048]{1,0:T(8,128)} async-done(((f32[256,2048]{1,0:T(8,128)}), f32[64,2048]{1,0:T(8,128)}) %reduce-scatter.3.cloned.1.call-update) | async-done | bytes 524304 | tf_op jit(solution)/shard_map/reduce_scatter | solution.py:62
  81.4 22.8 %all-gather.11.cloned.1.call-done = f32[128,2048]{1,0:T(8,128)} async-done(((f32[64,2048]{1,0:T(8,128)}), f32[128,2048]{1,0:T(8,128)}) %all-gather.11.cloned.1.call-update) | async-done | bytes 1048592 | tf_op jit(solution)/shard_map/all_gather | solution.py:71
  104.2 1.3 reduce_sum.85
  105.5 1.1 multiply_reduce_fusion
  106.6 1.8 multiply_convert_fusion.1
  108.4 3.6 %convolution_convert_fusion.1 = bf16[16,48,2048]{2,1,0:T(8,128)(2,1)} fusion(bf16[64,2048]{1,0:T(8,128)(2,1)} %multiply_convert_fusion.1, f32[16,64]{1,0:T(8,128)S(1)} %fusion.91, pred[16,64]{1,0:T(8,128)(4,1)S(1)} %compare_bitcast_fusion), kind=kOutput, calls=%fused_computation.2 | convolution fusion | flops 202997760 | bytes 3412992 | tf_op jit(solution)/shard_map/est,td->esd/dot_general | solution.py:166
  112.0 5.7 %all-to-all-start = ((bf16[16,48,2048]{2,1,0:T(8,128)(2,1)}), bf16[16,48,2048]{2,1,0:T(8,128)(2,1)}, u32[]{:S(2)}, u32[]{:S(2)}) async-start(bf16[16,48,2048]{2,1,0:T(8,128)(2,1)} %convolution_convert_fusion.1), calls=%async_computation.2 | async-start | bytes 6291456 | tf_op jit(solution)/shard_map/all_to_all | solution.py:169
  117.9 0.3 all-gather.9.cloned.1.call-update
  118.3 58.9 %all-to-all-done = bf16[16,48,2048]{2,1,0:T(8,128)(2,1)} async-done(((bf16[16,48,2048]{2,1,0:T(8,128)(2,1)}), bf16[16,48,2048]{2,1,0:T(8,128)(2,1)}, u32[]{:S(2)}, u32[]{:S(2)}) %all-to-all-start) | async-done | bytes 3145760 | tf_op jit(solution)/shard_map/all_to_all | solution.py:169
  177.2 5.2 %fusion.4 = f32[768,704]{0,1:T(8,128)S(1)} fusion(bf16[768,2048]{1,0:T(8,128)(2,1)} %bitcast.17, bf16[1,2,2048,704]{2,3,1,0:T(8,128)(2,1)} %param.36), kind=kOutput, calls=%fused_computation.6 | convolution fusion | flops 2214592512 | bytes 8192000 | tf_op jit(solution)/shard_map/dot_general | solution.py:177
  182.4 6.3 %multiply_convert_fusion = bf16[768,704]{0,1:T(8,128)(2,1)} fusion(f32[768,704]{0,1:T(8,128)S(1)} %fusion.4, bf16[768,2048]{1,0:T(8,128)(2,1)} %bitcast.17, bf16[1,2,2048,704]{2,3,1,0:T(8,128)(2,1)} %param.36), kind=kOutput, calls=%fused_computation.15 | convolution fusion | flops 2217836544 | bytes 9273344 | tf_op jit(solution)/shard_map/dot_general | solution.py:178
  188.7 2.4 copy.39
  191.1 5.3 %convolution_convert_fusion = bf16[16,48,2048]{2,1,0:T(8,128)(2,1)} fusion(bf16[16,48,704]{2,1,0:T(8,128)(2,1)} %bitcast.143, bf16[1,704,2048]{2,1,0:T(8,128)(2,1)S(1)} %copy-done), kind=kOutput, calls=%fused_computation.1 | convolution fusion | flops 2216165376 | bytes 7110656 | tf_op jit(solution)/shard_map/dot_general | solution.py:180
  196.3 15.5 %all-to-all-start.1 = ((bf16[16,48,2048]{2,1,0:T(8,128)(2,1)}), bf16[16,48,2048]{2,1,0:T(8,128)(2,1)}, u32[]{:S(2)}, u32[]{:S(2)}) async-start(bf16[16,48,2048]{2,1,0:T(8,128)(2,1)} %convolution_convert_fusion), calls=%async_computation.3 | async-start | bytes 6291456 | tf_op jit(solution)/shard_map/all_to_all | solution.py:183
  211.9 3.0 fusion.17
  214.9 5.6 %fusion.43 = f32[256,2048]{1,0:T(8,128)} fusion(bf16[352,2048]{1,0:T(8,128)(2,1)} %param.35, bf16[256,2048]{1,0:T(8,128)(2,1)} %all-gather.9.cloned.1.call-done, bf16[2,2048,352]{1,2,0:T(8,128)(2,1)} %param.34, f32[256,352]{0,1:T(8,128)} %fusion.17), kind=kOutput, calls=%fused_computation.38 | convolution fusion | flops 738738176 | bytes 6389760 | tf_op jit(solution)/shard_map/dot_general | solution.py:63
  220.6 1.1 fusion.112
  221.8 38.3 %reduce-scatter.5.cloned.1.call-done = f32[64,2048]{1,0:T(8,128)} async-done(((f32[256,2048]{1,0:T(8,128)}), f32[64,2048]{1,0:T(8,128)}) %reduce-scatter.5.cloned.1.call-update) | async-done | bytes 524304 | tf_op jit(solution)/shard_map/reduce_scatter | solution.py:62
  260.1 11.3 %all-to-all-done.1 = bf16[16,48,2048]{2,1,0:T(8,128)(2,1)} async-done(((bf16[16,48,2048]{2,1,0:T(8,128)(2,1)}), bf16[16,48,2048]{2,1,0:T(8,128)(2,1)}, u32[]{:S(2)}, u32[]{:S(2)}) %all-to-all-start.1) | async-done | bytes 3145760 | tf_op jit(solution)/shard_map/all_to_all | solution.py:183
  271.4 4.6 %fusion.8 = f32[64,2048]{1,0:T(8,128)} fusion(f32[64,2048]{1,0:T(8,128)} %reduce-scatter.5.cloned.1.call-done, bf16[16,48,2048]{2,1,0:T(8,128)(2,1)} %all-to-all-done.1, f32[16,64]{1,0:T(8,128)S(1)} %divide_bitcast_fusion, f32[16,64]{1,0:T(8,128)S(1)} %fusion.91, pred[16,64]{1,0:T(8,128)(4,1)} %copy-done.7), kind=kOutput, calls=%fused_computation.11 | convolution fusion | flops 1208238080 | bytes 4203520 | tf_op jit(solution)/shard_map/est,esd->td/dot_general | solution.py:187
  276.8 0.7 fusion.102
  277.5 1.7 fusion.46
  279.2 28.0 %all-gather.13.cloned.1.call-done = f32[128,2048]{1,0:T(8,128)} async-done(((f32[64,2048]{1,0:T(8,128)}), f32[128,2048]{1,0:T(8,128)}) %all-gather.13.cloned.1.call-update) | async-done | bytes 1048592 | tf_op jit(solution)/shard_map/all_gather | solution.py:71
  307.2 2.1 reduce_sum.89
  309.3 1.9 add_convert_fusion
  (56 shorter events, 1.7 us)
Async XLA Ops:
  7.2 183.9 %copy-start = (bf16[1,704,2048]{2,1,0:T(8,128)(2,1)S(1)}, bf16[1,704,2048]{2,1,0:T(8,128)(2,1)}, u32[]{:S(2)}) copy-start(bf16[1,704,2048]{2,1,0:T(8,128)(2,1)} %param.37) | copy-start | bytes 8650756
  7.2 22.8 %all-gather.7.cloned.1.call-start = ((), (), s32[]{:S(2)}) async-start(), calls=%async_computation.4 | async-start | bytes 1310720 | tf_op jit(solution)/shard_map/all_gather | solution.py:58
  10.3 6.1 %copy-start.10 = (s32[4]{0:T(128)S(1)}, s32[4]{0:T(128)}, u32[]{:S(2)}) copy-start(s32[4]{0:T(128)} %param.21) | copy-start | bytes 52
  10.3 70.9 %reduce-scatter.3.cloned.1.call-start = ((), (), s32[]{:S(2)}) async-start(), calls=%async_computation.5 | async-start | bytes 2621440 | tf_op jit(solution)/shard_map/reduce_scatter | solution.py:62
  32.6 3.1 copy-start.3
  32.7 3.2 %copy-start.9 = (f32[512]{0:T(512)S(1)}, f32[512]{0:T(512)}, u32[]{:S(2)}) copy-start(f32[512]{0:T(512)} %param.28) | copy-start | bytes 6148
  35.8 1.0 copy-start.6
  35.8 2.8 copy-start.1
  35.8 1.7 slice-start
  36.1 4.2 %copy-start.2 = (bf16[4,64,512]{2,1,0:T(8,128)(2,1)}, bf16[4,64,512]{2,1,0:T(8,128)(2,1)S(1)}, u32[]{:S(2)}) copy-start(bf16[4,64,512]{2,1,0:T(8,128)(2,1)S(1)} %multiply_convert_fusion.2) | copy-start | bytes 786436
  37.5 2.8 copy-start.4
  37.5 2.8 copy-start.5
  46.6 34.6 %copy-start.8 = (s32[64,6]{0,1:T(8,128)S(1)}, s32[64,6]{0,1:T(8,128)}, u32[]{:S(2)}) copy-start(s32[64,6]{0,1:T(8,128)} %param.23) | copy-start | bytes 4612
  49.6 54.5 %all-gather.11.cloned.1.call-start = ((), (), s32[]{:S(2)}) async-start(), calls=%async_computation.8 | async-start | bytes 1572864 | tf_op jit(solution)/shard_map/all_gather | solution.py:71
  81.3 30.8 %copy-start.7 = (pred[16,64]{1,0:T(8,128)(4,1)}, pred[16,64]{1,0:T(8,128)(4,1)S(1)}, u32[]{:S(2)}) copy-start(pred[16,64]{1,0:T(8,128)(4,1)S(1)} %compare_bitcast_fusion) | copy-start | bytes 3076
  112.0 65.1 %all-to-all-start = ((bf16[16,48,2048]{2,1,0:T(8,128)(2,1)}), bf16[16,48,2048]{2,1,0:T(8,128)(2,1)}, u32[]{:S(2)}, u32[]{:S(2)}) async-start(bf16[16,48,2048]{2,1,0:T(8,128)(2,1)} %convolution_convert_fusion.1), calls=%async_computation.2 | async-start | bytes 6291456 | tf_op jit(solution)/shard_map/all_to_all | solution.py:169
  117.7 94.2 %all-gather.9.cloned.1.call-start = ((), (), s32[]{:S(2)}) async-start(), calls=%async_computation.6 | async-start | bytes 1310720 | tf_op jit(solution)/shard_map/all_gather | solution.py:58
  196.3 75.0 %all-to-all-start.1 = ((bf16[16,48,2048]{2,1,0:T(8,128)(2,1)}), bf16[16,48,2048]{2,1,0:T(8,128)(2,1)}, u32[]{:S(2)}, u32[]{:S(2)}) async-start(bf16[16,48,2048]{2,1,0:T(8,128)(2,1)} %convolution_convert_fusion), calls=%async_computation.3 | async-start | bytes 6291456 | tf_op jit(solution)/shard_map/all_to_all | solution.py:183
  211.8 48.3 %reduce-scatter.5.cloned.1.call-start = ((), (), s32[]{:S(2)}) async-start(), calls=%async_computation.7 | async-start | bytes 2621440 | tf_op jit(solution)/shard_map/reduce_scatter | solution.py:62
  220.5 86.7 %all-gather.13.cloned.1.call-start = ((), (), s32[]{:S(2)}) async-start(), calls=%async_computation.9 | async-start | bytes 1572864 | tf_op jit(solution)/shard_map/all_gather | solution.py:71
Sparse Core Ops, SparseCore 0:
  10.4 19.5 all-gather.6
  49.8 31.3 reduce-scatter.2
  82.8 21.2 all-gather.10
  120.4 30.2 all-gather.8
  220.7 39.3 reduce-scatter.4
  276.1 31.0 all-gather.12
